TPU v7x, 32 devices: a whole 2x2x4 slice. The times are simulated.
32 devices in a mesh: dp: 16 (over z, y, core), tensor: 2 (over x).
Axes of the slice: x: 2, y: 2, z: 4, core: 2. Of those that a mesh axis runs over, the one named last changes fastest.
Arguments:
- tokens: bfloat16 [28672, 768], P(('dp', 'tensor')), may hold values from -6 to 6
- cotangent: bfloat16 [28672, 768], P(('dp', 'tensor')), may hold values from -6 to 6
- time_embed: float32 [16, 128], P('dp'), may hold values from -4 to 4
- block_parent: int32 [16, 14], P('dp'), may hold values from 0 to 5, as said below
- positions: int32 [28672], P('dp'), may hold values from 0 to 511, as said below
- gain_first: bfloat16 [768], P(('dp', 'tensor')), may hold values from 0.25 to 1.75
- inlet_weight: bfloat16 [768, 3, 12, 64], P('dp', None, 'tensor'), may hold values from -0.21875 to 0.21875
- outlet_weight: bfloat16 [12, 64, 768], P('tensor', None, 'dp'), may hold values from -0.875 to 0.875
- gain_second: bfloat16 [768], P(('dp', 'tensor')), may hold values from 0.25 to 1.75
- up_weight: bfloat16 [768, 3072], P(None, ('dp', 'tensor')), may hold values from -0.21875 to 0.21875
- up_bias: bfloat16 [3072], P(('dp', 'tensor')), may hold values from -3 to 3
- down_weight: bfloat16 [3072, 768], P(('dp', 'tensor')), may hold values from -0.109375 to 0.109375
- down_bias: bfloat16 [768], P(('dp', 'tensor')), may hold values from -2 to 2
- modulator: bfloat16 [128, 6, 768], P(None, None, ('dp', 'tensor')), may hold values from -0.5 to 0.5
- modulator_bias: bfloat16 [6, 768], P(None, ('dp', 'tensor')), may hold values from -3 to 3
Outputs:
- layer_output: bfloat16 [28672, 768], P(('dp', 'tensor'))
- adjoint_tokens: bfloat16 [28672, 768], P(('dp', 'tensor'))
- adjoint_gain_first: float32 [768], P(('dp', 'tensor'))
- adjoint_inlet: float32 [768, 3, 12, 64], P('dp', None, 'tensor')
- adjoint_outlet: float32 [12, 64, 768], P('tensor', None, 'dp')
- adjoint_gain_second: float32 [768], P(('dp', 'tensor'))
- adjoint_up_weight: float32 [768, 3072], P(None, ('dp', 'tensor'))
- adjoint_up_bias: float32 [3072], P(('dp', 'tensor'))
- adjoint_down_weight: float32 [3072, 768], P(('dp', 'tensor'))
- adjoint_down_bias: float32 [768], P(('dp', 'tensor'))
- adjoint_modulator: float32 [128, 6, 768], P(None, None, ('dp', 'tensor'))
- adjoint_modulator_bias: float32 [6, 768], P(None, ('dp', 'tensor'))
Inputs may be any that keep to these rules, and one draw needn't show every extreme that they name: block_parent[t, b] is the parent block of block b of tree t. Blocks 0 to 1 are the trunk: block 0 is its own parent and block b > 0 has parent b - 1. The next 4 blocks are branches, each with a trunk block as parent; the last 8 blocks are leaves, each with a branch block as parent. positions of a token = 128 times the number of strict ancestors of its block plus its place within its block.
All inputs are finite; a program needn't handle non-finite values.
Results may differ from a plain program's by a relative error of at most 0.02.
The roundings to bfloat16 on the way count: a program that leaves them out, or rounds other values in their place, can miss the bound.
Values may be sent and summed in bfloat16 or wider, within the bound.
No kernel may reach another device: no remote copies, remote signals or barrier semaphores. Data moves between devices by JAX's collectives and lax.ppermute only.
A program may use at most 192 MiB of HBM per device.

v0:
```python
from functools import partial
import jax
import jax.numpy as jnp
from jax import lax
from jax.sharding import PartitionSpec as P

EPS = 1e-05
ROPE_BASE = 10000.0
MASKED = -1e30
HIGHEST = lax.Precision.HIGHEST


def modulate(values, weight_gain, offset, stretch):
    center = values - jnp.mean(values, axis=-1, keepdims=True)
    second = jnp.mean(center * center, axis=-1, keepdims=True)
    return center * lax.rsqrt(second + EPS) * weight_gain * (1.0 + stretch) + offset


def rotary_tables(places, width):
    halfway = width // 2
    inverse = ROPE_BASE ** (-(jnp.arange(halfway, dtype=jnp.float32) * 2.0 / width))
    angles = places.astype(jnp.float32)[:, None] * inverse[None, :]
    return (jnp.cos(angles), jnp.sin(angles))


def rotate(vectors, cosine, sine_part):
    halfway = vectors.shape[-1] // 2
    former = vectors[..., :halfway]
    latter = vectors[..., halfway:]
    cosine = cosine[:, None, :]
    sine_part = sine_part[:, None, :]
    return jnp.concatenate(
        [former * cosine - latter * sine_part, latter * cosine + former * sine_part], axis=-1
    )


def path_mask(parents, length):
    amount = parents.shape[0]
    labels = jnp.arange(amount, dtype=jnp.int32)
    climb_map = (parents[:, None] == labels[None, :]).astype(jnp.float32)
    identity = jnp.eye(amount, dtype=jnp.float32)

    def climb(iteration, carried):
        reached, ancestry = carried
        reached = jnp.dot(reached, climb_map, precision=HIGHEST)
        return (reached, jnp.maximum(ancestry, reached))

    reached, ancestry = lax.fori_loop(0, amount, climb, (identity, identity))
    linked = jnp.maximum(ancestry, ancestry.T)
    owners = jnp.arange(length, dtype=jnp.int32) // (length // amount)
    chooser = (owners[:, None] == labels[None, :]).astype(jnp.float32)
    joined = jnp.dot(jnp.dot(chooser, linked, precision=HIGHEST), chooser.T, precision=HIGHEST)
    return joined > 0.5


def head_order(array):
    return jnp.transpose(array, (1, 0, 2))


def fetch_layer(inlet_weight, outlet_weight, up_weight, down_weight, up_bias):
    return (
        lax.all_gather(inlet_weight, "dp", axis=0, tiled=True),
        lax.all_gather(outlet_weight, "dp", axis=2, tiled=True),
        lax.all_gather(up_weight, "dp", axis=1, tiled=True),
        lax.all_gather(down_weight, "dp", axis=0, tiled=True),
        lax.all_gather(up_bias, "dp", axis=0, tiled=True),
    )


def head_forward(allowed, scale_factor, bundle):
    queries, keys_rot, values_v = bundle
    scores = jnp.dot(queries, keys_rot.T, preferred_element_type=jnp.float32)
    logits = jnp.where(allowed, scores * scale_factor, MASKED)
    highest = jnp.max(logits, axis=-1, keepdims=True)
    raised = jnp.exp(logits - highest)
    totals = jnp.sum(raised, axis=-1, keepdims=True)
    probs = raised / totals
    attended = jnp.dot(probs.astype(jnp.bfloat16), values_v, preferred_element_type=jnp.float32)
    return (attended.astype(jnp.bfloat16), (highest + jnp.log(totals))[:, 0])


def head_backward(allowed, scale_factor, bundle):
    queries, keys_rot, values_v, slope, log_total = bundle
    scores = jnp.dot(queries, keys_rot.T, preferred_element_type=jnp.float32)
    logits = jnp.where(allowed, scores * scale_factor, MASKED)
    probs = jnp.exp(logits - log_total[:, None])
    value_adj = jnp.dot(probs.astype(jnp.bfloat16).T, slope, preferred_element_type=jnp.float32)
    prob_slope = jnp.dot(slope, values_v.T, preferred_element_type=jnp.float32)
    inner = jnp.sum(probs * prob_slope, axis=-1, keepdims=True)
    score_slope = (probs * (prob_slope - inner) * scale_factor).astype(jnp.bfloat16)
    query_adj = jnp.dot(score_slope, keys_rot, preferred_element_type=jnp.float32)
    key_adj = jnp.dot(score_slope.T, queries, preferred_element_type=jnp.float32)
    return (query_adj, key_adj, value_adj)


def per_device(
    tokens,
    cotangent,
    time_embed,
    block_parent,
    positions,
    gain_first,
    inlet_weight,
    outlet_weight,
    gain_second,
    up_weight,
    up_bias,
    down_weight,
    down_bias,
    modulator,
    modulator_bias,
):
    smalls = (
        lax.all_gather(gain_first, ("dp", "tensor"), axis=0, tiled=True),
        lax.all_gather(gain_second, ("dp", "tensor"), axis=0, tiled=True),
        lax.all_gather(down_bias, ("dp", "tensor"), axis=0, tiled=True),
        lax.all_gather(modulator_bias, ("dp", "tensor"), axis=1, tiled=True),
        lax.all_gather(modulator, ("dp", "tensor"), axis=2, tiled=True),
    )
    norm_one, norm_two, bias_down, bias_mod, weight_mod = [
        member.astype(jnp.float32) for member in smalls
    ]
    width = tokens.shape[1]
    inlet_full, outlet_full, up_full, down_full, up_bias_full = fetch_layer(
        inlet_weight, outlet_weight, up_weight, down_weight, up_bias
    )
    local_heads = inlet_full.shape[2]
    head_width = inlet_full.shape[3]
    inlet_flat = inlet_full.reshape(width, -1)
    outlet_flat = outlet_full.reshape(local_heads * head_width, width)
    embed_act = jax.nn.silu(time_embed)
    shifts = (
        jnp.dot(embed_act, weight_mod.reshape(weight_mod.shape[0], -1), precision=HIGHEST).reshape(
            6, width
        )
        + bias_mod
    )
    values = tokens.astype(jnp.float32)
    normed = modulate(values, norm_one, shifts[0], shifts[1]).astype(jnp.bfloat16)
    normed_all = lax.all_gather(normed, "tensor", axis=0, tiled=True)
    length = normed_all.shape[0]
    mixed = jnp.dot(normed_all, inlet_flat, preferred_element_type=jnp.float32).reshape(
        length, 3, local_heads, head_width
    )
    cosine, sine_part = rotary_tables(positions, head_width)
    queries = head_order(rotate(mixed[:, 0], cosine, sine_part).astype(jnp.bfloat16))
    keys_rot = head_order(rotate(mixed[:, 1], cosine, sine_part).astype(jnp.bfloat16))
    values_v = head_order(mixed[:, 2].astype(jnp.bfloat16))
    allowed = path_mask(block_parent[0], length)
    scale_factor = head_width ** (-0.5)
    attended_heads, log_totals = lax.map(
        partial(head_forward, allowed, scale_factor), (queries, keys_rot, values_v)
    )
    attended = head_order(attended_heads).reshape(length, local_heads * head_width)
    branch_part = jnp.dot(attended, outlet_flat, preferred_element_type=jnp.float32)
    branch = lax.psum_scatter(
        branch_part.astype(jnp.bfloat16), "tensor", scatter_dimension=0, tiled=True
    ).astype(jnp.float32)
    middle = values + shifts[2] * branch
    normed_two = modulate(middle, norm_two, shifts[3], shifts[4]).astype(jnp.bfloat16)
    normed_two_all = lax.all_gather(normed_two, "tensor", axis=0, tiled=True)
    hidden = jnp.dot(
        normed_two_all, up_full, preferred_element_type=jnp.float32
    ) + up_bias_full.astype(jnp.float32)
    activated = jax.nn.gelu(hidden, approximate=True).astype(jnp.bfloat16)
    mlp_part = jnp.dot(activated, down_full, preferred_element_type=jnp.float32)
    mlp_out = lax.psum_scatter(
        mlp_part.astype(jnp.bfloat16), "tensor", scatter_dimension=0, tiled=True
    ).astype(jnp.float32)
    layer_output = (middle + shifts[5] * (mlp_out + bias_down)).astype(jnp.bfloat16)
    inlet_full, outlet_full, up_full, down_full, up_bias_full = fetch_layer(
        inlet_weight, outlet_weight, up_weight, down_weight, up_bias
    )
    inlet_flat = inlet_full.reshape(width, -1)
    outlet_flat = outlet_full.reshape(local_heads * head_width, width)
    slope = cotangent.astype(jnp.float32)
    gate_two_adj = jnp.sum(slope * (mlp_out + bias_down), axis=0)
    down_bias_adj = jnp.sum(slope, axis=0) * shifts[5]
    mlp_slope = (slope * shifts[5]).astype(jnp.bfloat16)
    mlp_slope_all = lax.all_gather(mlp_slope, "tensor", axis=0, tiled=True)
    down_adj = jnp.dot(activated.T, mlp_slope_all, preferred_element_type=jnp.float32)
    act_slope = jnp.dot(mlp_slope_all, down_full.T, preferred_element_type=jnp.float32)
    gelu_back = jax.vjp(partial(jax.nn.gelu, approximate=True), hidden)[1]
    hidden_slope = gelu_back(act_slope)[0].astype(jnp.bfloat16)
    up_bias_adj = jnp.sum(hidden_slope.astype(jnp.float32), axis=0)
    up_adj = jnp.dot(normed_two_all.T, hidden_slope, preferred_element_type=jnp.float32)
    norm_two_part = jnp.dot(hidden_slope, up_full.T, preferred_element_type=jnp.float32)
    norm_two_slope = lax.psum_scatter(
        norm_two_part.astype(jnp.bfloat16), "tensor", scatter_dimension=0, tiled=True
    ).astype(jnp.float32)
    middle_back = jax.vjp(modulate, middle, norm_two, shifts[3], shifts[4])[1]
    middle_adj, gain_two_adj, shift_two_adj, scale_two_adj = middle_back(norm_two_slope)
    middle_slope = slope + middle_adj
    gate_one_adj = jnp.sum(middle_slope * branch, axis=0)
    branch_slope = (middle_slope * shifts[2]).astype(jnp.bfloat16)
    branch_slope_all = lax.all_gather(branch_slope, "tensor", axis=0, tiled=True)
    outlet_adj = jnp.dot(attended.T, branch_slope_all, preferred_element_type=jnp.float32)
    attended_slope = jnp.dot(
        branch_slope_all, outlet_flat.T, preferred_element_type=jnp.float32
    ).astype(jnp.bfloat16)
    attended_slope = head_order(attended_slope.reshape(length, local_heads, head_width))
    query_adj, key_adj, value_adj = lax.map(
        partial(head_backward, allowed, scale_factor),
        (queries, keys_rot, values_v, attended_slope, log_totals),
    )
    query_adj = rotate(head_order(query_adj), cosine, -sine_part)
    key_adj = rotate(head_order(key_adj), cosine, -sine_part)
    mixed_slope = (
        jnp.stack([query_adj, key_adj, head_order(value_adj)], axis=1)
        .astype(jnp.bfloat16)
        .reshape(length, -1)
    )
    inlet_adj = jnp.dot(normed_all.T, mixed_slope, preferred_element_type=jnp.float32).reshape(
        width, 3, local_heads, head_width
    )
    normed_part = jnp.dot(mixed_slope, inlet_flat.T, preferred_element_type=jnp.float32)
    normed_slope = lax.psum_scatter(
        normed_part.astype(jnp.bfloat16), "tensor", scatter_dimension=0, tiled=True
    ).astype(jnp.float32)
    values_back = jax.vjp(modulate, values, norm_one, shifts[0], shifts[1])[1]
    values_adj, gain_one_adj, shift_one_adj, scale_one_adj = values_back(normed_slope)
    adjoint_tokens = (middle_slope + values_adj).astype(jnp.bfloat16)
    shift_adj = jnp.stack(
        [shift_one_adj, scale_one_adj, gate_one_adj, shift_two_adj, scale_two_adj, gate_two_adj]
    )
    mod_weight_adj = embed_act[0][:, None, None] * shift_adj[None]
    outlet_adj = outlet_adj.reshape(local_heads, head_width, width)
    inlet_share, outlet_share, up_share, down_share, up_bias_share = (
        lax.psum_scatter(inlet_adj, "dp", scatter_dimension=0, tiled=True),
        lax.psum_scatter(outlet_adj, "dp", scatter_dimension=2, tiled=True),
        lax.psum_scatter(up_adj, "dp", scatter_dimension=1, tiled=True),
        lax.psum_scatter(down_adj, "dp", scatter_dimension=0, tiled=True),
        lax.psum_scatter(up_bias_adj, "dp", scatter_dimension=0, tiled=True),
    )
    gain_one_share, gain_two_share, down_bias_share, mod_bias_share, mod_weight_share = (
        lax.psum_scatter(gain_one_adj, ("dp", "tensor"), scatter_dimension=0, tiled=True),
        lax.psum_scatter(gain_two_adj, ("dp", "tensor"), scatter_dimension=0, tiled=True),
        lax.psum_scatter(down_bias_adj, ("dp", "tensor"), scatter_dimension=0, tiled=True),
        lax.psum_scatter(shift_adj, ("dp", "tensor"), scatter_dimension=1, tiled=True),
        lax.psum_scatter(mod_weight_adj, ("dp", "tensor"), scatter_dimension=2, tiled=True),
    )
    return (
        layer_output,
        adjoint_tokens,
        gain_one_share,
        inlet_share,
        outlet_share,
        gain_two_share,
        up_share,
        up_bias_share,
        down_share,
        down_bias_share,
        mod_weight_share,
        mod_bias_share,
    )


def solution(mesh):
    in_specs = (
        P(("dp", "tensor"), None),
        P(("dp", "tensor"), None),
        P("dp", None),
        P("dp", None),
        P("dp"),
        P(("dp", "tensor")),
        P("dp", None, "tensor", None),
        P("tensor", None, "dp"),
        P(("dp", "tensor")),
        P(None, ("dp", "tensor")),
        P(("dp", "tensor")),
        P(("dp", "tensor"), None),
        P(("dp", "tensor")),
        P(None, None, ("dp", "tensor")),
        P(None, ("dp", "tensor")),
    )
    out_specs = (
        P(("dp", "tensor"), None),
        P(("dp", "tensor"), None),
        P(("dp", "tensor")),
        P("dp", None, "tensor", None),
        P("tensor", None, "dp"),
        P(("dp", "tensor")),
        P(None, ("dp", "tensor")),
        P(("dp", "tensor")),
        P(("dp", "tensor"), None),
        P(("dp", "tensor")),
        P(None, None, ("dp", "tensor")),
        P(None, ("dp", "tensor")),
    )
    return jax.shard_map(
        per_device, mesh=mesh, in_specs=in_specs, out_specs=out_specs, check_vma=False
    )
```

profile of v0, /device:TPU:0, one launch (start us, length us, event | category | flops | bytes accessed | tf_op | source)
XLA Modules:
  0.0 1269.2 jit_solution(4032610746774366570)
XLA Ops:
  11.3 42.1 %all-reduce.10 = (bf16[768]{0:T(1024)(128)(2,1)}, bf16[768]{0:T(1024)(128)(2,1)S(1)}, bf16[768]{0:T(1024)(128)(2,1)}) all-reduce(bf16[768]{0:T(1024)(128)(2,1)S(1)} %dynamic-update-slice.1, bf16[768]{0:T(1024)(128)(2,1)S(1)} %dynamic-update-slice, ...), channel_id=1, replica_groups=mesh['dp'=16,'tensor'=2] {'dp','tensor'}, use_global_device_ids=true, to_apply=%add.1 | all-reduce | flops 2304 | bytes 9216
  53.4 67.6 %all-gather = bf16[32,24,6]{1,2,0:T(8,128)(2,1)S(1)} all-gather(bf16[1,24,6]{1,2,0:T(8,128)(2,1)} %bitcast.206), channel_id=1, replica_groups=mesh['dp'=16,'tensor'=2] {'dp','tensor'}, dimensions={0}, use_global_device_ids=true | all-gather | bytes 9504 | tf_op jit(solution)/shard_map/all_gather | solution.py:117
  132.3 7.7 convolution_compare_fusion
  143.4 22.4 %all_gather.51 = bf16[6,64,768]{1,2,0:T(8,128)(2,1)} all-gather(bf16[6,64,48]{1,2,0:T(8,128)(2,1)S(1)} %copy-done.23), channel_id=1, replica_groups=mesh['dp'=16,'tensor'=2] {'dp'}, dimensions={2}, use_global_device_ids=true | all-gather | bytes 626688 | tf_op jit(solution)/shard_map/all_gather | solution.py:63
  167.5 4.8 copy.71
  172.3 5.7 fusion.83
  182.8 3.9 copy.73
  186.7 3.9 copy.76
  190.6 4.0 copy.74
  194.6 59.2 %while.39 = (s32[]{:T(128)}, bf16[6,1792,64]{1,2,0:T(8,128)(2,1)}, f32[6,1792]{1,0:T(8,128)S(1)}, bf16[6,1792,64]{2,1,0:T(8,128)(2,1)}, bf16[6,1792,64]{2,1,0:T(...) while((s32[]{:T(128)}, bf16[6,1792,64]{1,2,0:T(8,128)(2,1)}, ...), condition=%wide.region_7.8_spmd, body=%wide.region_4.7_spmd.sunk | while | flops 847886592 | bytes 43440232 | solution.py:151
  200.1 4.2 fusion.157
  209.9 4.2 fusion.157
  219.8 4.2 fusion.157
  229.7 4.2 fusion.157
  239.6 4.2 fusion.157
  249.4 4.2 fusion.157
  253.9 5.6 bitcast_convert_fusion.1
  260.6 35.3 %reduce-scatter.11.cloned.1.call-done = bf16[896,768]{1,0:T(8,128)(2,1)} async-done(((bf16[1792,768]{1,0:T(8,128)(2,1)}), bf16[896,768]{1,0:T(8,128)(2,1)}) %reduce-scatter.11.cloned.1.call-update) | async-done | bytes 1376272 | tf_op jit(solution)/shard_map/reduce_scatter | solution.py:156
  306.4 33.3 %all-reduce.2 = bf16[1536]{0:T(1024)(128)(2,1)S(1)} all-reduce(bf16[1536]{0:T(1024)(128)(2,1)S(1)} %dynamic-update-slice.2), channel_id=1, replica_groups=mesh['dp'=16,'tensor'=2] {'dp'}, use_global_device_ids=true, to_apply=%add.2 | all-reduce | flops 1536 | bytes 6144
  340.6 41.2 %all-gather.16.cloned.1.call-done = bf16[1792,768]{1,0:T(8,128)(2,1)} async-done(((bf16[896,768]{1,0:T(8,128)(2,1)}), bf16[1792,768]{1,0:T(8,128)(2,1)}) %all-gather.16.cloned.1.call-update) | async-done | bytes 2752528 | tf_op jit(solution)/shard_map/all_gather | solution.py:161
  381.7 12.3 multiply_convert_fusion.1
  394.0 32.4 %all-gather.20.cloned.1.call-done = bf16[1536,768]{1,0:T(8,128)(2,1)} async-done(((bf16[96,768]{1,0:T(8,128)(2,1)}), bf16[1536,768]{1,0:T(8,128)(2,1)}) %all-gather.20.cloned.1.call-update) | async-done | bytes 2359312 | tf_op jit(solution)/shard_map/all_gather | solution.py:65
  426.4 40.8 %all-gather.22.cloned.1.call-done = bf16[1792,768]{1,0:T(8,128)(2,1)} async-done(((bf16[896,768]{1,0:T(8,128)(2,1)}), bf16[1792,768]{1,0:T(8,128)(2,1)}) %all-gather.22.cloned.1.call-update) | async-done | bytes 2752528 | tf_op jit(solution)/shard_map/all_gather | solution.py:180
  467.1 15.4 %convert_reduce_fusion = (f32[1536]{0:T(1024)}, bf16[1792,1536]{1,0:T(8,128)(2,1)S(1)}) fusion(f32[1792,1536]{1,0:T(8,128)} %get-tuple-element.307, f32[1536]{0:T(1024)S(1)} %convert_element_type.125, bf16[1792,768]{1,0:T(8,128)(2,1)} %all-gather.22.cloned.1.call-done, bf16[1536,768]{1,0:T(8,128)(2,1)} %all-gather.20.cloned.1.call-done), kind=kOutput, calls=%fused_computation.63 | convolution fusion | flops 4291164672 | bytes 21639168 | tf_op jit(solution)/shard_map/dot_general | solution.py:182
  484.9 5.7 convolution_convert_fusion
  490.8 9.3 convolution_convert_fusion.1
  500.8 29.1 %reduce-scatter.15.cloned.1.call-done = bf16[896,768]{1,0:T(8,128)(2,1)} async-done(((bf16[1792,768]{1,0:T(8,128)(2,1)}), bf16[896,768]{1,0:T(8,128)(2,1)}) %reduce-scatter.15.cloned.1.call-update) | async-done | bytes 1376272 | tf_op jit(solution)/shard_map/reduce_scatter | solution.py:188
  535.9 35.1 %reduce-scatter.13.cloned.1.call-done = bf16[896,768]{1,0:T(8,128)(2,1)} async-done(((bf16[1792,768]{1,0:T(8,128)(2,1)}), bf16[896,768]{1,0:T(8,128)(2,1)}) %reduce-scatter.13.cloned.1.call-update) | async-done | bytes 1376272 | tf_op jit(solution)/shard_map/reduce_scatter | solution.py:167
  571.0 6.1 fusion.75
  582.6 38.1 %all-gather.24.cloned.1.call-done = bf16[1792,768]{1,0:T(8,128)(2,1)} async-done(((bf16[896,768]{1,0:T(8,128)(2,1)}), bf16[1792,768]{1,0:T(8,128)(2,1)}) %all-gather.24.cloned.1.call-update) | async-done | bytes 2752528 | tf_op jit(solution)/shard_map/all_gather | solution.py:196
  620.7 4.3 convolution_convert_fusion.2
  625.0 3.9 copy.78
  628.9 154.9 %while.40 = (s32[]{:T(128)}, f32[6,1792,64]{1,2,0:T(8,128)}, f32[6,1792,64]{1,2,0:T(8,128)}, bf16[6,1792,64]{1,2,0:T(8,128)(2,1)}, bf16[6,1792,64]{2,1,0:T(8,128...) while((s32[]{:T(128)}, f32[6,1792,64]{1,2,0:T(8,128)}, ...), condition=%wide.region_17.18_spmd, body=%wide.region_15.17_spmd.sunk | while | flops 2087319808 | bytes 155558096 | solution.py:202
  633.6 6.2 multiply_reduce_fusion.3
  639.8 3.8 multiply_convert_fusion.4
  643.6 3.9 fusion.169
  647.6 3.9 fusion.168
  659.3 6.2 multiply_reduce_fusion.3
  665.5 3.8 multiply_convert_fusion.4
  669.4 4.0 fusion.169
  673.3 3.9 fusion.168
  685.2 6.2 multiply_reduce_fusion.3
  695.2 4.0 fusion.169
  699.2 3.9 fusion.168
  711.0 6.2 multiply_reduce_fusion.3
  721.0 3.9 fusion.169
  725.0 3.9 fusion.168
  736.8 6.2 multiply_reduce_fusion.3
  746.8 4.0 fusion.169
  750.8 3.9 fusion.168
  762.6 6.2 multiply_reduce_fusion.3
  772.7 4.0 fusion.169
  776.6 3.9 fusion.168
  789.7 8.5 bitcast_convert_fusion
  798.2 10.0 fusion.114
  808.4 10.1 fusion.115
  818.7 6.0 fusion.85
  824.8 10.4 fusion.55
  844.1 33.7 %all-reduce.6 = f32[1536]{0:T(1024)S(1)} all-reduce(f32[1536]{0:T(1024)S(1)} %copy-done.38), channel_id=11, replica_groups=mesh['dp'=16,'tensor'=2] {'dp'}, use_global_device_ids=true, to_apply=%region_29.30.clone | all-reduce | flops 1536 | bytes 12288
  878.5 39.2 %all-reduce.9 = (f32[768]{0:T(1024)S(1)}, f32[768]{0:T(1024)S(1)}, f32[768]{0:T(1024)S(1)}, f32[6,768]{1,0:T(8,128)S(1)}) all-reduce(f32[768]{0:T(1024)S(1)} %get-tuple-element.216, f32[768]{0:T(1024)S(1)} %copy-done.33, f32[768]{0:T(1024)S(1)} %mul.488, ...), channel_id=6, replica_groups=mesh['dp'=16,'tensor'=2] {'dp','tensor'}, use_global_device_ids=true, to_apply=%region_22.23.clone | all-reduce | flops 6912 | bytes 55296
  923.6 73.9 %reduce-scatter.25.cloned.1.call-done = f32[96,768]{1,0:T(8,128)} async-done(((f32[1536,768]{1,0:T(8,128)}), f32[96,768]{1,0:T(8,128)}) %reduce-scatter.25.cloned.1.call-update) | async-done | bytes 294928 | tf_op jit(solution)/shard_map/reduce_scatter | solution.py:232
  997.5 66.6 %reduce-scatter.21.cloned.1.call-done = f32[6,64,48]{1,2,0:T(8,128)} async-done(((f32[6,64,768]{1,2,0:T(8,128)}), f32[6,64,48]{1,2,0:T(8,128)}) %reduce-scatter.21.cloned.1.call-update) | async-done | bytes 73744 | tf_op jit(solution)/shard_map/reduce_scatter | solution.py:230
  1064.1 93.3 %reduce-scatter.19.cloned.1.call-done = f32[48,3,6,64]{3,0,2,1:T(8,128)} async-done(((f32[768,3,6,64]{3,0,2,1:T(8,128)}), f32[48,3,6,64]{3,0,2,1:T(8,128)}) %reduce-scatter.19.cloned.1.call-update) | async-done | bytes 221200 | tf_op jit(solution)/shard_map/reduce_scatter | solution.py:229
  1157.5 105.0 %reduce-scatter.27.cloned.1.call-done = f32[128,6,24]{0,2,1:T(8,128)} async-done(((f32[128,6,768]{0,2,1:T(8,128)}), f32[128,6,24]{0,2,1:T(8,128)}) %reduce-scatter.27.cloned.1.call-update) | async-done | bytes 73744 | tf_op jit(solution)/shard_map/reduce_scatter | solution.py:240
  (326 shorter events, 171.8 us)
Async XLA Ops:
  7.2 115.8 %copy-start.3 = (bf16[896,768]{1,0:T(8,128)(2,1)S(1)}, bf16[896,768]{1,0:T(8,128)(2,1)}, u32[]{:S(2)}) copy-start(bf16[896,768]{1,0:T(8,128)(2,1)} %param.21) | copy-start | bytes 4128772
  7.2 116.4 %copy-start.42 = (f32[1,128]{1,0:T(1,128)S(1)}, f32[1,128]{1,0:T(1,128)}, u32[]{:S(2)}) copy-start(f32[1,128]{1,0:T(1,128)} %param.23) | copy-start | bytes 1540
  7.2 116.4 %all-gather.10.cloned.1.call-start = ((), (), s32[]{:S(2)}) async-start(), calls=%async_computation.9 | async-start | bytes 1216512 | tf_op jit(solution)/shard_map/all_gather | solution.py:118
  7.9 159.6 %all-gather.14.cloned.1.call-start = ((), (), s32[]{:S(2)}) async-start(), calls=%async_computation.11 | async-start | bytes 3760128 | tf_op jit(solution)/shard_map/all_gather | solution.py:62
  8.7 163.6 %all-gather.12.cloned.1.call-start = ((), (), s32[]{:S(2)}) async-start(), calls=%async_computation.10 | async-start | bytes 4128768 | tf_op jit(solution)/shard_map/all_gather | solution.py:140
  53.4 74.9 %copy-start.18 = (f32[768]{0:T(1024)}, f32[768]{0:T(1024)S(1)}, u32[]{:S(2)}) copy-start(f32[768]{0:T(1024)S(1)} %convert_element_type.115) | copy-start | bytes 9220
  123.0 5.3 copy-start.16
  123.5 5.0 copy-start.28
  123.5 5.0 copy-start.46
  123.5 5.0 copy-start.26
  123.5 8.1 copy-start.37
  126.5 5.8 copy-start.20
  128.3 167.6 %reduce-scatter.11.cloned.1.call-start = ((), (), s32[]{:S(2)}) async-start(), calls=%async_computation.12 | async-start | bytes 4128768 | tf_op jit(solution)/shard_map/reduce_scatter | solution.py:156
  140.0 3.4 copy-start.23
  167.5 12.1 copy-start.13
  259.5 36.4 %copy-start.15 = (f32[768]{0:T(1024)S(1)}, f32[768]{0:T(1024)}, u32[]{:S(2)}) copy-start(f32[768]{0:T(1024)} %get-tuple-element.226) | copy-start | bytes 9220
  259.5 81.0 %all-gather.18.cloned.1.call-start = ((), (), s32[]{:S(2)}) async-start(), calls=%async_computation.14 | async-start | bytes 2506752 | tf_op jit(solution)/shard_map/all_gather | solution.py:64
  260.1 121.6 %all-gather.16.cloned.1.call-start = ((), (), s32[]{:S(2)}) async-start(), calls=%async_computation.13 | async-start | bytes 4128768 | tf_op jit(solution)/shard_map/all_gather | solution.py:161
  295.9 2.5 copy-start.4
  295.9 2.6 copy-start.7
  295.9 3.4 copy-start.22
  295.9 3.4 copy-start.36
  299.3 2.8 copy-start.24
  301.3 3.6 copy-start.41
  301.3 4.9 copy-start.47
  301.3 125.0 %all-gather.20.cloned.1.call-start = ((), (), s32[]{:S(2)}) async-start(), calls=%async_computation.15 | async-start | bytes 2506752 | tf_op jit(solution)/shard_map/all_gather | solution.py:65
  302.1 165.1 %all-gather.22.cloned.1.call-start = ((), (), s32[]{:S(2)}) async-start(), calls=%async_computation.17 | async-start | bytes 4128768 | tf_op jit(solution)/shard_map/all_gather | solution.py:180
  304.8 225.0 %reduce-scatter.15.cloned.1.call-start = ((), (), s32[]{:S(2)}) async-start(), calls=%async_computation.18 | async-start | bytes 4128768 | tf_op jit(solution)/shard_map/reduce_scatter | solution.py:188
  467.1 17.8 %copy-start.44 = (bf16[768,1536]{0,1:T(8,128)(2,1)S(1)}, bf16[768,1536]{0,1:T(8,128)(2,1)}, u32[]{:S(2)}) copy-start(bf16[768,1536]{0,1:T(8,128)(2,1)} %all-gather.18.cloned.1.call-done) | copy-start | bytes 7077892
  482.5 2.4 copy-start.48
  490.6 80.5 %reduce-scatter.13.cloned.1.call-start = ((), (), s32[]{:S(2)}) async-start(), calls=%async_computation.16 | async-start | bytes 4128768 | tf_op jit(solution)/shard_map/reduce_scatter | solution.py:167
  500.1 120.6 %all-gather.24.cloned.1.call-start = ((), (), s32[]{:S(2)}) async-start(), calls=%async_computation.19 | async-start | bytes 4128768 | tf_op jit(solution)/shard_map/all_gather | solution.py:196
  529.8 3.4 copy-start.5
  529.8 3.4 copy-start.8
  529.8 3.4 copy-start.11
  580.1 257.4 %reduce-scatter.17.cloned.1.call-start = ((), (), s32[]{:S(2)}) async-start(), calls=%async_computation.20 | async-start | bytes 4128768 | tf_op jit(solution)/shard_map/reduce_scatter | solution.py:217
  643.6 3.9 copy-start
  651.4 3.2 copy-start.2
  669.4 4.0 copy-start
  677.2 3.2 copy-start.2
  695.2 4.0 copy-start
  703.1 3.3 copy-start.2
  721.0 3.9 copy-start
  728.9 3.2 copy-start.2
  746.8 4.0 copy-start
  754.7 3.2 copy-start.2
  772.7 4.0 copy-start
  780.5 3.3 copy-start.2
  787.3 2.4 copy-start.45
  798.2 125.4 %reduce-scatter.23.cloned.1.call-start = ((), (), s32[]{:S(2)}) async-start(), calls=%async_computation.23 | async-start | bytes 5013504 | tf_op jit(solution)/shard_map/reduce_scatter | solution.py:231
  808.3 189.2 %reduce-scatter.25.cloned.1.call-start = ((), (), s32[]{:S(2)}) async-start(), calls=%async_computation.24 | async-start | bytes 5013504 | tf_op jit(solution)/shard_map/reduce_scatter | solution.py:232
  818.5 245.7 %reduce-scatter.21.cloned.1.call-start = ((), (), s32[]{:S(2)}) async-start(), calls=%async_computation.22 | async-start | bytes 2506752 | tf_op jit(solution)/shard_map/reduce_scatter | solution.py:230
  824.7 332.8 %reduce-scatter.19.cloned.1.call-start = ((), (), s32[]{:S(2)}) async-start(), calls=%async_computation.21 | async-start | bytes 7520256 | tf_op jit(solution)/shard_map/reduce_scatter | solution.py:229
  835.2 2.3 copy-start.6
  835.2 2.2 copy-start.17
  835.2 2.2 copy-start.19
  835.3 4.4 copy-start.29
  835.3 4.5 copy-start.27
  835.3 427.2 %reduce-scatter.27.cloned.1.call-start = ((), (), s32[]{:S(2)}) async-start(), calls=%async_computation.25 | async-start | bytes 2433024 | tf_op jit(solution)/shard_map/reduce_scatter | solution.py:240
  837.5 2.3 copy-start.10
  841.5 2.6 copy-start.38
  841.5 36.9 %copy-start.25 = (f32[768]{0:T(1024)S(1)}, f32[768]{0:T(1024)}, u32[]{:S(2)}) copy-start(f32[768]{0:T(1024)} %get-tuple-element.221) | copy-start | bytes 9220
  841.6 36.9 %copy-start.30 = (f32[768]{0:T(1024)S(1)}, f32[768]{0:T(1024)}, u32[]{:S(2)}) copy-start(f32[768]{0:T(1024)} %get-tuple-element.295) | copy-start | bytes 9220
  841.6 36.9 %copy-start.33 = (f32[768]{0:T(1024)S(1)}, f32[768]{0:T(1024)}, u32[]{:S(2)}) copy-start(f32[768]{0:T(1024)} %get-tuple-element.213) | copy-start | bytes 9220
  (17 other events, 21.9 us)
Sparse Core Ops, SparseCore 0:
  10.9 54.4 all-gather.9
  67.6 47.3 all-gather.13
  128.4 36.3 all-gather.11
  259.6 36.2 reduce-scatter.10
  298.1 42.4 all-gather.17
  342.5 39.1 all-gather.15
  384.0 42.3 all-gather.19
  427.9 39.1 all-gather.21
  490.7 39.0 reduce-scatter.14
  531.9 39.0 reduce-scatter.12
  580.2 40.4 all-gather.23
  798.3 39.0 reduce-scatter.16
  841.9 76.5 reduce-scatter.22
  922.7 74.7 reduce-scatter.24
  1001.7 62.4 reduce-scatter.20
  1068.6 88.8 reduce-scatter.18
  1163.2 99.2 reduce-scatter.26
where the time goes:
time: 1270 us
  waiting for transfers between devices  596 us (47%)
  matrix products  285 us (22%)
  blocking collectives  238 us (19%)
  other arithmetic  77.1 us (6%)
  local copies, waits for them, and re-layouts  54.1 us (4%)
  between operations  16.2 us (1%)
    unnamed x4, blocking collectives  148 us
    reduce_scatter x1, waiting for transfers between devices, per_device(): lax.psum_scatter(mod_weight_adj, ('dp', 'tensor'), scatter_dimension=2, t...  105 us
    reduce_scatter x1, waiting for transfers between devices, per_device(): lax.psum_scatter(inlet_adj, 'dp', scatter_dimension=0, tiled=True)  93.3 us
    reduce_scatter x1, waiting for transfers between devices, per_device(): lax.psum_scatter(down_adj, 'dp', scatter_dimension=0, tiled=True)  73.9 us
    all_gather x1, blocking collectives, per_device(): lax.all_gather(modulator_bias, ('dp', 'tensor'), axis=1, tiled=True)  67.6 us
    reduce_scatter x1, waiting for transfers between devices, per_device(): lax.psum_scatter(outlet_adj, 'dp', scatter_dimension=2, tiled=True)  66.6 us
    all_gather x1, waiting for transfers between devices, per_device(): normed_two_all = lax.all_gather(normed_two, 'tensor', axis=0, tiled=True)  41.2 us
    all_gather x1, waiting for transfers between devices, per_device(): mlp_slope_all = lax.all_gather(mlp_slope, 'tensor', axis=0, tiled=True)  40.8 us
  transfers between devices with their start and end apart: 17, of which 13 were waited for; matrix products, arithmetic and copies ran while one was open for 9% of the time, Pallas kernels for 0%

commit v1 on v0

--- a/solution.py
+++ b/solution.py
@@ -8,6 +8,24 @@
 ROPE_BASE = 10000.0
 MASKED = -1e30
 HIGHEST = lax.Precision.HIGHEST
+
+
+def laid_out(pieces, dim):
+    pieces = jnp.moveaxis(pieces, 0, dim)
+    lengths = pieces.shape
+    return pieces.reshape(*lengths[:dim], lengths[dim] * lengths[dim + 1], *lengths[dim + 2 :])
+
+
+def grow_blocks(value, axis):
+    size = lax.axis_size(axis)
+    parts = value[None]
+    for level in range(size.bit_length() - 1):
+        stride = 1 << level
+        other = lax.ppermute(parts, axis, [(i, i ^ stride) for i in range(size)])
+        both = jnp.stack([parts, other])
+        upper = lax.axis_index(axis) >> level & 1
+        parts = jnp.where(upper == 0, both, both[::-1]).reshape(-1, *value.shape)
+    return parts
 
 
 def modulate(values, weight_gain, offset, stretch):
@@ -158,7 +176,7 @@
     ).astype(jnp.float32)
     middle = values + shifts[2] * branch
     normed_two = modulate(middle, norm_two, shifts[3], shifts[4]).astype(jnp.bfloat16)
-    normed_two_all = lax.all_gather(normed_two, "tensor", axis=0, tiled=True)
+    normed_two_all = laid_out(grow_blocks(normed_two, "tensor"), 0)
     hidden = jnp.dot(
         normed_two_all, up_full, preferred_element_type=jnp.float32
     ) + up_bias_full.astype(jnp.float32)

time: 1270 us -> 1230 us (0.969)
  waiting for transfers between devices: 596 us -> 547 us
    all_gather x1 -> x0, waiting for transfers between devices: 41.2 us -> none  [per_device(): normed_two_all = lax.all_gather(normed_two, 'tensor', axis=0, tiled=True)]
  transfers between devices with their start and end apart: 17 -> 17, of which waited for: 13 -> 10; matrix products, arithmetic and copies ran while one was open for 9% -> 10% of each run, Pallas kernels for 0% -> 0%
where the time goes in v1:
time: 1230 us
  waiting for transfers between devices  547 us (44%)
  matrix products  284 us (23%)
  blocking collectives  238 us (19%)
  other arithmetic  80.4 us (7%)
  local copies, waits for them, and re-layouts  59 us (5%)
  between operations  16.2 us (1%)
    unnamed x4, blocking collectives  148 us
    reduce_scatter x1, waiting for transfers between devices, per_device(): lax.psum_scatter(mod_weight_adj, ('dp', 'tensor'), scatter_dimension=2, t...  105 us
    reduce_scatter x1, waiting for transfers between devices, per_device(): lax.psum_scatter(inlet_adj, 'dp', scatter_dimension=0, tiled=True)  93.3 us
    reduce_scatter x1, waiting for transfers between devices, per_device(): lax.psum_scatter(down_adj, 'dp', scatter_dimension=0, tiled=True)  73.2 us
    all_gather x1, blocking collectives, per_device(): lax.all_gather(modulator_bias, ('dp', 'tensor'), axis=1, tiled=True)  67.5 us
    reduce_scatter x1, waiting for transfers between devices, per_device(): lax.psum_scatter(outlet_adj, 'dp', scatter_dimension=2, tiled=True)  66.6 us
    all_gather x1, waiting for transfers between devices, per_device(): mlp_slope_all = lax.all_gather(mlp_slope, 'tensor', axis=0, tiled=True)  40.8 us
    all_gather x1, waiting for transfers between devices, per_device(): lax.all_gather(branch_slope, 'tensor', axis=0, tiled=True)  38.1 us
  transfers between devices with their start and end apart: 17, of which 10 were waited for; matrix products, arithmetic and copies ran while one was open for 10% of the time, Pallas kernels for 0%

profile of v1, /device:TPU:0, one launch (start us, length us, event | category | flops | bytes accessed | tf_op | source)
XLA Modules:
  0.0 1227.4 jit_solution(3400326489492390829)
XLA Ops:
  11.3 42.2 %all-reduce.10 = (bf16[768]{0:T(1024)(128)(2,1)}, bf16[768]{0:T(1024)(128)(2,1)S(1)}, bf16[768]{0:T(1024)(128)(2,1)}) all-reduce(bf16[768]{0:T(1024)(128)(2,1)S(1)} %dynamic-update-slice.1, bf16[768]{0:T(1024)(128)(2,1)S(1)} %dynamic-update-slice, ...), channel_id=1, replica_groups=mesh['dp'=16,'tensor'=2] {'dp','tensor'}, use_global_device_ids=true, to_apply=%add.1 | all-reduce | flops 2304 | bytes 9216
  53.5 67.5 %all-gather = bf16[32,24,6]{1,2,0:T(8,128)(2,1)S(1)} all-gather(bf16[1,24,6]{1,2,0:T(8,128)(2,1)} %bitcast.214), channel_id=1, replica_groups=mesh['dp'=16,'tensor'=2] {'dp','tensor'}, dimensions={0}, use_global_device_ids=true | all-gather | bytes 9504 | tf_op jit(solution)/shard_map/all_gather | solution.py:135
  132.3 7.7 convolution_compare_fusion
  143.4 22.4 %all_gather.48 = bf16[6,64,768]{1,2,0:T(8,128)(2,1)} all-gather(bf16[6,64,48]{1,2,0:T(8,128)(2,1)S(1)} %copy-done.29), channel_id=1, replica_groups=mesh['dp'=16,'tensor'=2] {'dp'}, dimensions={2}, use_global_device_ids=true | all-gather | bytes 626688 | tf_op jit(solution)/shard_map/all_gather | solution.py:81
  167.5 4.8 copy.71
  172.2 5.7 fusion.83
  182.7 3.9 copy.73
  186.6 3.9 copy.76
  190.6 3.9 copy.74
  194.5 59.2 %while.39 = (s32[]{:T(128)}, bf16[6,1792,64]{1,2,0:T(8,128)(2,1)}, f32[6,1792]{1,0:T(8,128)S(1)}, bf16[6,1792,64]{2,1,0:T(8,128)(2,1)}, bf16[6,1792,64]{2,1,0:T(...) while((s32[]{:T(128)}, bf16[6,1792,64]{1,2,0:T(8,128)(2,1)}, ...), condition=%wide.region_7.8_spmd, body=%wide.region_4.7_spmd.sunk | while | flops 847886592 | bytes 43440232 | solution.py:169
  199.9 4.2 fusion.159
  209.8 4.2 fusion.159
  219.7 4.2 fusion.159
  229.6 4.2 fusion.159
  239.4 4.2 fusion.159
  249.3 4.2 fusion.159
  253.7 5.7 bitcast_convert_fusion.1
  261.1 34.8 %reduce-scatter.11.cloned.1.call-done = bf16[896,768]{1,0:T(8,128)(2,1)} async-done(((bf16[1792,768]{1,0:T(8,128)(2,1)}), bf16[896,768]{1,0:T(8,128)(2,1)}) %reduce-scatter.11.cloned.1.call-update) | async-done | bytes 1376272 | tf_op jit(solution)/shard_map/reduce_scatter | solution.py:174
  305.1 33.6 %all-reduce.2 = bf16[1536]{0:T(1024)(128)(2,1)S(1)} all-reduce(bf16[1536]{0:T(1024)(128)(2,1)S(1)} %dynamic-update-slice.2), channel_id=1, replica_groups=mesh['dp'=16,'tensor'=2] {'dp'}, use_global_device_ids=true, to_apply=%add.2 | all-reduce | flops 1536 | bytes 6144
  342.8 12.3 %multiply_convert_fusion.1 = (bf16[1792,1536]{1,0:T(8,128)(2,1)}, f32[1792,1536]{1,0:T(8,128)}) fusion(f32[1536]{0:T(1024)S(1)} %convert_element_type.125, bf16[1792,768]{1,0:T(8,128)(2,1)} %bitcast.208, bf16[768,1536]{0,1:T(8,128)(2,1)} %all-gather.15.cloned.1.call-done), kind=kOutput, calls=%fused_computation.64 | convolution fusion | flops 4255383552 | bytes 21633024 | tf_op jit(solution)/shard_map/dot_general | solution.py:180
  355.2 28.3 %all-gather.17.cloned.1.call-done = bf16[1536,768]{1,0:T(8,128)(2,1)} async-done(((bf16[96,768]{1,0:T(8,128)(2,1)}), bf16[1536,768]{1,0:T(8,128)(2,1)}) %all-gather.17.cloned.1.call-update) | async-done | bytes 2359312 | tf_op jit(solution)/shard_map/all_gather | solution.py:83
  383.5 40.8 %all-gather.19.cloned.1.call-done = bf16[1792,768]{1,0:T(8,128)(2,1)} async-done(((bf16[896,768]{1,0:T(8,128)(2,1)}), bf16[1792,768]{1,0:T(8,128)(2,1)}) %all-gather.19.cloned.1.call-update) | async-done | bytes 2752528 | tf_op jit(solution)/shard_map/all_gather | solution.py:198
  424.3 15.4 %convert_reduce_fusion = (f32[1536]{0:T(1024)}, bf16[1792,1536]{1,0:T(8,128)(2,1)S(1)}) fusion(f32[1792,1536]{1,0:T(8,128)} %get-tuple-element.309, f32[1536]{0:T(1024)S(1)} %convert_element_type.125, bf16[1792,768]{1,0:T(8,128)(2,1)} %all-gather.19.cloned.1.call-done, bf16[1536,768]{1,0:T(8,128)(2,1)} %all-gather.17.cloned.1.call-done), kind=kOutput, calls=%fused_computation.63 | convolution fusion | flops 4291164672 | bytes 21639168 | tf_op jit(solution)/shard_map/dot_general | solution.py:200
  442.0 5.7 convolution_convert_fusion
  447.9 9.3 convolution_convert_fusion.1
  457.9 29.1 %reduce-scatter.15.cloned.1.call-done = bf16[896,768]{1,0:T(8,128)(2,1)} async-done(((bf16[1792,768]{1,0:T(8,128)(2,1)}), bf16[896,768]{1,0:T(8,128)(2,1)}) %reduce-scatter.15.cloned.1.call-update) | async-done | bytes 1376272 | tf_op jit(solution)/shard_map/reduce_scatter | solution.py:206
  493.1 35.3 %reduce-scatter.13.cloned.1.call-done = bf16[896,768]{1,0:T(8,128)(2,1)} async-done(((bf16[1792,768]{1,0:T(8,128)(2,1)}), bf16[896,768]{1,0:T(8,128)(2,1)}) %reduce-scatter.13.cloned.1.call-update) | async-done | bytes 1376272 | tf_op jit(solution)/shard_map/reduce_scatter | solution.py:185
  528.4 6.1 fusion.75
  539.9 38.1 %all-gather.21.cloned.1.call-done = bf16[1792,768]{1,0:T(8,128)(2,1)} async-done(((bf16[896,768]{1,0:T(8,128)(2,1)}), bf16[1792,768]{1,0:T(8,128)(2,1)}) %all-gather.21.cloned.1.call-update) | async-done | bytes 2752528 | tf_op jit(solution)/shard_map/all_gather | solution.py:214
  578.1 4.3 convolution_convert_fusion.2
  582.3 3.9 copy.78
  586.2 154.8 %while.40 = (s32[]{:T(128)}, f32[6,1792,64]{1,2,0:T(8,128)}, f32[6,1792,64]{1,2,0:T(8,128)}, bf16[6,1792,64]{1,2,0:T(8,128)(2,1)}, bf16[6,1792,64]{2,1,0:T(8,128...) while((s32[]{:T(128)}, f32[6,1792,64]{1,2,0:T(8,128)}, ...), condition=%wide.region_17.18_spmd, body=%wide.region_15.17_spmd.sunk | while | flops 2087319808 | bytes 155558096 | solution.py:220
  590.9 6.2 multiply_reduce_fusion.3
  597.1 3.8 multiply_convert_fusion.4
  600.9 3.9 fusion.171
  604.9 3.9 fusion.170
  616.7 6.2 multiply_reduce_fusion.3
  622.9 3.8 multiply_convert_fusion.4
  626.7 4.0 fusion.171
  630.7 3.9 fusion.170
  642.5 6.2 multiply_reduce_fusion.3
  648.7 3.8 multiply_convert_fusion.4
  652.6 3.9 fusion.171
  656.5 3.9 fusion.170
  668.3 6.2 multiply_reduce_fusion.3
  678.3 3.9 fusion.171
  682.3 3.9 fusion.170
  694.1 6.2 multiply_reduce_fusion.3
  704.1 3.9 fusion.171
  708.0 3.9 fusion.170
  719.9 6.2 multiply_reduce_fusion.3
  729.9 3.9 fusion.171
  733.8 3.9 fusion.170
  747.9 8.5 bitcast_convert_fusion
  758.2 9.3 fusion.116
  769.2 9.2 fusion.117
  778.7 6.2 fusion.85
  785.0 10.3 fusion.55
  803.4 34.1 %all-reduce.6 = f32[1536]{0:T(1024)S(1)} all-reduce(f32[1536]{0:T(1024)S(1)} %copy-done.44), channel_id=11, replica_groups=mesh['dp'=16,'tensor'=2] {'dp'}, use_global_device_ids=true, to_apply=%region_29.30.clone | all-reduce | flops 1536 | bytes 12288
  838.1 38.4 %all-reduce.9 = (f32[768]{0:T(1024)S(1)}, f32[768]{0:T(1024)S(1)}, f32[768]{0:T(1024)S(1)}, f32[6,768]{1,0:T(8,128)S(1)}) all-reduce(f32[768]{0:T(1024)S(1)} %get-tuple-element.216, f32[768]{0:T(1024)S(1)} %copy-done.39, f32[768]{0:T(1024)S(1)} %mul.488, ...), channel_id=6, replica_groups=mesh['dp'=16,'tensor'=2] {'dp','tensor'}, use_global_device_ids=true, to_apply=%region_22.23.clone | all-reduce | flops 6912 | bytes 55296
  882.4 73.2 %reduce-scatter.25.cloned.1.call-done = f32[96,768]{1,0:T(8,128)} async-done(((f32[1536,768]{1,0:T(8,128)}), f32[96,768]{1,0:T(8,128)}) %reduce-scatter.25.cloned.1.call-update) | async-done | bytes 294928 | tf_op jit(solution)/shard_map/reduce_scatter | solution.py:250
  955.7 66.6 %reduce-scatter.21.cloned.1.call-done = f32[6,64,48]{1,2,0:T(8,128)} async-done(((f32[6,64,768]{1,2,0:T(8,128)}), f32[6,64,48]{1,2,0:T(8,128)}) %reduce-scatter.21.cloned.1.call-update) | async-done | bytes 73744 | tf_op jit(solution)/shard_map/reduce_scatter | solution.py:248
  1022.3 93.3 %reduce-scatter.19.cloned.1.call-done = f32[48,3,6,64]{3,0,2,1:T(8,128)} async-done(((f32[768,3,6,64]{3,0,2,1:T(8,128)}), f32[48,3,6,64]{3,0,2,1:T(8,128)}) %reduce-scatter.19.cloned.1.call-update) | async-done | bytes 221200 | tf_op jit(solution)/shard_map/reduce_scatter | solution.py:247
  1115.6 105.1 %reduce-scatter.27.cloned.1.call-done = f32[128,6,24]{0,2,1:T(8,128)} async-done(((f32[128,6,768]{0,2,1:T(8,128)}), f32[128,6,24]{0,2,1:T(8,128)}) %reduce-scatter.27.cloned.1.call-update) | async-done | bytes 73744 | tf_op jit(solution)/shard_map/reduce_scatter | solution.py:258
  (341 shorter events, 174.1 us)
Async XLA Ops:
  7.2 115.7 %copy-start.3 = (bf16[896,768]{1,0:T(8,128)(2,1)S(1)}, bf16[896,768]{1,0:T(8,128)(2,1)}, u32[]{:S(2)}) copy-start(bf16[896,768]{1,0:T(8,128)(2,1)} %param.21) | copy-start | bytes 4128772
  7.2 116.3 %copy-start.48 = (f32[1,128]{1,0:T(1,128)S(1)}, f32[1,128]{1,0:T(1,128)}, u32[]{:S(2)}) copy-start(f32[1,128]{1,0:T(1,128)} %param.23) | copy-start | bytes 1540
  7.2 116.3 %all-gather.9.cloned.1.call-start = ((), (), s32[]{:S(2)}) async-start(), calls=%async_computation.9 | async-start | bytes 1216512 | tf_op jit(solution)/shard_map/all_gather | solution.py:136
  7.9 159.5 %all-gather.13.cloned.1.call-start = ((), (), s32[]{:S(2)}) async-start(), calls=%async_computation.11 | async-start | bytes 3760128 | tf_op jit(solution)/shard_map/all_gather | solution.py:80
  8.7 163.6 %all-gather.11.cloned.1.call-start = ((), (), s32[]{:S(2)}) async-start(), calls=%async_computation.10 | async-start | bytes 4128768 | tf_op jit(solution)/shard_map/all_gather | solution.py:158
  53.4 74.8 %copy-start.24 = (f32[768]{0:T(1024)}, f32[768]{0:T(1024)S(1)}, u32[]{:S(2)}) copy-start(f32[768]{0:T(1024)S(1)} %convert_element_type.115) | copy-start | bytes 9220
  122.9 5.4 copy-start.22
  123.4 5.1 copy-start.34
  123.4 5.0 copy-start.53
  123.5 5.0 copy-start.32
  123.5 8.1 copy-start.43
  126.5 5.8 copy-start.26
  128.3 167.6 %reduce-scatter.11.cloned.1.call-start = ((), (), s32[]{:S(2)}) async-start(), calls=%async_computation.12 | async-start | bytes 4128768 | tf_op jit(solution)/shard_map/reduce_scatter | solution.py:174
  139.9 3.4 copy-start.29
  167.5 12.2 copy-start.15
  259.4 36.4 %copy-start.21 = (f32[768]{0:T(1024)S(1)}, f32[768]{0:T(1024)}, u32[]{:S(2)}) copy-start(f32[768]{0:T(1024)} %get-tuple-element.226) | copy-start | bytes 9220
  259.4 83.4 %all-gather.15.cloned.1.call-start = ((), (), s32[]{:S(2)}) async-start(), calls=%async_computation.13 | async-start | bytes 2506752 | tf_op jit(solution)/shard_map/all_gather | solution.py:82
  260.0 123.5 %all-gather.17.cloned.1.call-start = ((), (), s32[]{:S(2)}) async-start(), calls=%async_computation.14 | async-start | bytes 2506752 | tf_op jit(solution)/shard_map/all_gather | solution.py:83
  260.6 163.7 %all-gather.19.cloned.1.call-start = ((), (), s32[]{:S(2)}) async-start(), calls=%async_computation.16 | async-start | bytes 4128768 | tf_op jit(solution)/shard_map/all_gather | solution.py:198
  295.8 2.5 copy-start.4
  295.8 2.6 copy-start.7
  295.8 3.3 copy-start.28
  295.8 3.3 copy-start.42
  299.2 2.8 copy-start.12
  299.2 2.8 copy-start.30
  301.7 3.2 copy-start.54
  301.7 37.0 %collective-permute-start = (bf16[1,896,768]{2,1,0:T(8,128)(2,1)}, bf16[1,896,768]{2,1,0:T(8,128)(2,1)}, u32[]{:S(2)}, u32[]{:S(2)}) collective-permute-start(bf16[1,896,768]{2,1,0:T(8,128)(2,1)} %get-tuple-element.295), channel_id=1, source_target_pairs={{0,1},{1,0},{2,3},{3,2},{4,5},{5,4},{6,7},{7,6},{8,9},{9,8},{10,11... | collective-permute-start | bytes 4128776 | tf_op jit(solution)/shard_map/ppermute | solution.py:24
  303.5 183.5 %reduce-scatter.15.cloned.1.call-start = ((), (), s32[]{:S(2)}) async-start(), calls=%async_computation.17 | async-start | bytes 4128768 | tf_op jit(solution)/shard_map/reduce_scatter | solution.py:206
  424.3 17.8 %copy-start.51 = (bf16[768,1536]{0,1:T(8,128)(2,1)S(1)}, bf16[768,1536]{0,1:T(8,128)(2,1)}, u32[]{:S(2)}) copy-start(bf16[768,1536]{0,1:T(8,128)(2,1)} %all-gather.15.cloned.1.call-done) | copy-start | bytes 7077892
  439.6 2.4 copy-start.55
  447.7 80.7 %reduce-scatter.13.cloned.1.call-start = ((), (), s32[]{:S(2)}) async-start(), calls=%async_computation.15 | async-start | bytes 4128768 | tf_op jit(solution)/shard_map/reduce_scatter | solution.py:185
  457.2 120.8 %all-gather.21.cloned.1.call-start = ((), (), s32[]{:S(2)}) async-start(), calls=%async_computation.18 | async-start | bytes 4128768 | tf_op jit(solution)/shard_map/all_gather | solution.py:214
  487.0 3.4 copy-start.5
  487.0 3.4 copy-start.8
  487.0 3.4 copy-start.11
  537.4 258.6 %reduce-scatter.17.cloned.1.call-start = ((), (), s32[]{:S(2)}) async-start(), calls=%async_computation.19 | async-start | bytes 4128768 | tf_op jit(solution)/shard_map/reduce_scatter | solution.py:235
  600.9 3.9 copy-start
  608.8 3.2 copy-start.2
  626.7 4.0 copy-start
  634.6 3.3 copy-start.2
  652.6 3.9 copy-start
  660.4 3.3 copy-start.2
  678.3 3.9 copy-start
  686.1 3.2 copy-start.2
  704.1 3.9 copy-start
  711.9 3.2 copy-start.2
  729.9 3.9 copy-start
  737.7 3.3 copy-start.2
  744.5 3.0 copy-start.13
  744.5 3.4 copy-start.52
  756.4 126.0 %reduce-scatter.23.cloned.1.call-start = ((), (), s32[]{:S(2)}) async-start(), calls=%async_computation.22 | async-start | bytes 5013504 | tf_op jit(solution)/shard_map/reduce_scatter | solution.py:249
  767.5 188.2 %reduce-scatter.25.cloned.1.call-start = ((), (), s32[]{:S(2)}) async-start(), calls=%async_computation.23 | async-start | bytes 5013504 | tf_op jit(solution)/shard_map/reduce_scatter | solution.py:250
  778.5 6.5 copy-start.17
  778.5 6.5 copy-start.19
  778.5 243.8 %reduce-scatter.21.cloned.1.call-start = ((), (), s32[]{:S(2)}) async-start(), calls=%async_computation.21 | async-start | bytes 2506752 | tf_op jit(solution)/shard_map/reduce_scatter | solution.py:248
  784.9 330.7 %reduce-scatter.19.cloned.1.call-start = ((), (), s32[]{:S(2)}) async-start(), calls=%async_computation.20 | async-start | bytes 7520256 | tf_op jit(solution)/shard_map/reduce_scatter | solution.py:247
  795.4 3.6 copy-start.35
  795.4 3.6 copy-start.33
  795.4 425.2 %reduce-scatter.27.cloned.1.call-start = ((), (), s32[]{:S(2)}) async-start(), calls=%async_computation.24 | async-start | bytes 2433024 | tf_op jit(solution)/shard_map/reduce_scatter | solution.py:258
  796.7 2.3 copy-start.10
  800.8 2.6 copy-start.44
  800.8 37.3 %copy-start.31 = (f32[768]{0:T(1024)S(1)}, f32[768]{0:T(1024)}, u32[]{:S(2)}) copy-start(f32[768]{0:T(1024)} %get-tuple-element.221) | copy-start | bytes 9220
  800.8 37.3 %copy-start.36 = (f32[768]{0:T(1024)S(1)}, f32[768]{0:T(1024)}, u32[]{:S(2)}) copy-start(f32[768]{0:T(1024)} %get-tuple-element.297) | copy-start | bytes 9220
  800.8 37.3 %copy-start.39 = (f32[768]{0:T(1024)S(1)}, f32[768]{0:T(1024)}, u32[]{:S(2)}) copy-start(f32[768]{0:T(1024)} %get-tuple-element.213) | copy-start | bytes 9220
  (24 other events, 31.7 us)
Sparse Core Ops, SparseCore 0:
  10.9 54.4 all-gather.8
  67.6 47.3 all-gather.12
  128.4 36.3 all-gather.10
  259.6 36.2 reduce-scatter.10
  298.0 42.2 all-gather.14
  342.4 41.0 all-gather.16
  385.0 39.1 all-gather.18
  447.8 39.0 reduce-scatter.14
  489.2 39.0 reduce-scatter.12
  537.6 40.4 all-gather.20
  756.5 39.0 reduce-scatter.16
  800.0 76.4 reduce-scatter.22
  880.9 74.7 reduce-scatter.24
  959.9 62.4 reduce-scatter.20
  1026.7 88.8 reduce-scatter.18
  1121.3 99.2 reduce-scatter.26
